TPU v7x, 512 devices: a whole 4x4x16 slice. The times are simulated.
512 devices in a mesh: blk: 16 (over y, x_hi, core), group: 32 (over x_lo, z).
Axes of the slice: x: 4 (x_hi: 2, x_lo: 2; x = x_hi * 2 + x_lo), y: 4, z: 16, core: 2. Of those that a mesh axis runs over, the one named last changes fastest.
Arguments:
- student_features: bfloat16 [65536, 768], P(('blk', 'group')), may hold values from -8 to 8
- teacher_image: bfloat16 [65536, 1152], P(('blk', 'group')), may hold values from -8 to 8
- text_embeds: bfloat16 [65536, 1152], P(('blk', 'group')), may hold values from -8 to 8
- pair_ids: int32 [65536], replicated, may hold values from 0 to 8191
- head_weights: bfloat16 [1152, 768], replicated, may hold values from -1 to 1
- moment_first: float32 [1152, 768], P('group'), may hold values from -4 to 4
- moment_second: float32 [1152, 768], P('group'), may hold values from 0.01 to 0.3
Outputs:
- row_loss: float32 [65536], P(('blk', 'group'))
- new_first: float32 [1152, 768], P('group')
- new_second: float32 [1152, 768], P('group')
- new_weights: bfloat16 [1152, 768], replicated
All inputs are finite; a program needn't handle non-finite values.
Results may differ from a plain program's by a relative error of at most 0.0025.
The roundings to bfloat16 on the way count: a program that leaves them out, or rounds other values in their place, can miss the bound.
Values may be sent and summed in bfloat16 or wider, within the bound.
No kernel may reach another device: no remote copies, remote signals or barrier semaphores. Data moves between devices by JAX's collectives and lax.ppermute only.
A program may use at most 64 MiB of HBM per device.

v0:
```python
import jax
import jax.numpy as jnp
from jax import lax
from jax.sharding import PartitionSpec as P

student_scale = 20.0
student_bias = -1.0
teacher_scale = 25.0
teacher_bias = -1.5
label_mix = 0.5
norm_eps = 1e-06
beta_one = 0.9
beta_two = 0.95
learn_rate = 0.01
weight_decay = 0.0001
adam_eps = 1e-08
adam_step = 100.0


def from_partner(shard, axis, bit):
    return lax.ppermute(shard, axis, [(i, i ^ 1 << bit) for i in range(lax.axis_size(axis))])


def unit_rows(values):
    values = values.astype(jnp.float32)
    return values * lax.rsqrt(jnp.sum(values * values, axis=-1, keepdims=True) + norm_eps)


def pair_terms(student_rows, teacher_rows, left_ids, text_rows, right_ids):
    dims = (((1,), (1,)), ((), ()))
    student_logit = (
        student_scale
        * lax.dot_general(student_rows, text_rows, dims, preferred_element_type=jnp.float32)
        + student_bias
    )
    teacher_logit = (
        teacher_scale
        * lax.dot_general(teacher_rows, text_rows, dims, preferred_element_type=jnp.float32)
        + teacher_bias
    )
    labels = (left_ids[:, None] == right_ids[None, :]).astype(jnp.float32)
    target = (1.0 - label_mix) * labels + label_mix * jax.nn.sigmoid(teacher_logit)
    losses = jnp.sum(jax.nn.softplus(student_logit) - target * student_logit, axis=1)
    coeff = (jax.nn.sigmoid(student_logit) - target).astype(jnp.bfloat16)
    pulled = jnp.dot(coeff, text_rows, preferred_element_type=jnp.float32)
    return (losses, pulled)


def per_device(
    student_features,
    teacher_image,
    text_embeds,
    pair_ids,
    head_weights,
    moment_first,
    moment_second,
):
    row_count = student_features.shape[0]
    blk_count = lax.axis_size("blk")
    group_count = lax.axis_size("group")
    swap_bit = group_count.bit_length() - 2
    group_index = lax.axis_index("group")
    partner_index = (group_index + group_count // 2) % group_count
    blk_index = lax.axis_index("blk")
    projected = lax.dot_general(
        student_features, head_weights, (((1,), (1,)), ((), ())), preferred_element_type=jnp.float32
    )
    inverse = lax.rsqrt(jnp.sum(projected * projected, axis=-1, keepdims=True) + norm_eps)
    student = projected * inverse
    student_b = student.astype(jnp.bfloat16)
    teacher_b = unit_rows(teacher_image).astype(jnp.bfloat16)
    texts_b = unit_rows(text_embeds).astype(jnp.bfloat16)
    ids_grid = pair_ids.reshape(blk_count, group_count, row_count)
    own_ids = lax.dynamic_index_in_dim(ids_grid, group_index, 1, keepdims=False)
    far_ids = lax.dynamic_index_in_dim(ids_grid, partner_index, 1, keepdims=False)
    left_ids = lax.dynamic_index_in_dim(own_ids, blk_index, 0, keepdims=False)
    far_block = from_partner(texts_b, "group", swap_bit)
    paired = jnp.concatenate([texts_b, far_block], axis=0)
    paired_ids = jnp.stack([own_ids, far_ids], axis=1).reshape(-1)
    losses, pulled = pair_terms(
        student_b,
        teacher_b,
        left_ids,
        lax.all_gather(paired, "blk", axis=0, tiled=True),
        paired_ids,
    )
    totals = (losses, pulled)
    losses, pulled = totals
    row_loss = losses / row_count
    grad_student = student_scale / row_count * pulled
    grad_projected = (
        inverse * (grad_student - student * jnp.sum(student * grad_student, axis=-1, keepdims=True))
    ).astype(jnp.bfloat16)
    shard_rows = moment_first.shape[0]
    group_grad = lax.psum_scatter(
        lax.dot_general(
            grad_projected,
            student_features,
            (((0,), (0,)), ((), ())),
            preferred_element_type=jnp.float32,
        ),
        "group",
        scatter_dimension=0,
        tiled=True,
    )
    head_grad = lax.psum(group_grad, "blk")
    new_first = beta_one * moment_first + (1.0 - beta_one) * head_grad
    new_second = beta_two * moment_second + (1.0 - beta_two) * head_grad * head_grad
    first_hat = new_first / (1.0 - beta_one**adam_step)
    second_hat = new_second / (1.0 - beta_two**adam_step)
    own_weights = lax.dynamic_slice_in_dim(
        head_weights, group_index * shard_rows, shard_rows, 0
    ).astype(jnp.float32)
    updated = own_weights - learn_rate * (
        first_hat / (jnp.sqrt(second_hat) + adam_eps) + weight_decay * own_weights
    )
    new_weights = lax.all_gather(updated.astype(jnp.bfloat16), "group", axis=0, tiled=True)
    return (row_loss, new_first, new_second, new_weights)


def solution(mesh):
    placed = (
        P(("blk", "group"), None),
        P(("blk", "group"), None),
        P(("blk", "group"), None),
        P(),
        P(),
        P("group", None),
        P("group", None),
    )
    return jax.shard_map(
        per_device,
        mesh=mesh,
        in_specs=placed,
        out_specs=(P(("blk", "group")), P("group", None), P("group", None), P()),
        check_vma=False,
    )
```

profile of v0, /device:TPU:8, one launch (start us, length us, event | category | flops | bytes accessed | tf_op | source)
XLA Modules:
  0.0 531.9 jit_solution(12891333635255561007)
XLA Ops:
  7.2 0.0 copy-start
  7.2 0.0 copy-start.2
  7.2 0.0 copy-start.1
  7.2 0.0 all-gather.4.cloned.1.call-start
  7.2 1.3 fusion.12
  8.5 1.1 fusion.13
  9.6 3.4 collective-permute-start
  13.0 7.2 %collective-permute-done = bf16[128,1152]{1,0:T(8,128)(2,1)S(1)} collective-permute-done((bf16[128,1152]{1,0:T(8,128)(2,1)S(1)}, bf16[128,1152]{1,0:T(8,128)(2,1)S(1)}, u32[]{:S(2)}, u32[]{:S(2)}) %collective-permute-start) | collective-permute-done | bytes 294944 | tf_op jit(solution)/shard_map/ppermute | solution.py:21
  20.2 0.9 pad_maximum_fusion
  21.1 0.0 all-gather.4.cloned.1.call-update
  21.1 0.0 all-reduce.4.cloned.1.call-start
  21.2 0.7 fusion.27
  21.9 0.9 constant_dynamic-slice_fusion.2
  22.8 0.0 copy-done.2
  22.8 0.1 fusion.14
  23.0 0.0 copy-done
  23.0 0.0 copy-done.1
  23.0 0.8 multiply_reduce_fusion.1
  23.8 93.0 %all-gather.4.cloned.1.call-done = bf16[4096,1152]{1,0:T(8,128)(2,1)} async-done(((bf16[256,1152]{1,0:T(8,128)(2,1)}), bf16[4096,1152]{1,0:T(8,128)(2,1)}) %all-gather.4.cloned.1.call-update) | async-done | bytes 9437200 | tf_op jit(solution)/shard_map/all_gather | solution.py:84
  116.8 0.0 copy-start.5
  116.8 7.1 %fusion.8 = f32[128,4096]{1,0:T(8,128)S(1)} fusion(bf16[4096,1152]{1,0:T(8,128)(2,1)} %all-gather.4.cloned.1.call-done, s32[4096]{0:T(1024)S(1)} %bitcast.15, s32[128]{0:T(128)S(1)} %fusion.27, bf16[128,1152]{1,0:T(8,128)(2,1)S(1)} %copy-done.2, f32[128]{0:T(128)S(1)} %add_rsqrt_fusion), kind=kOutput, calls=%fused_computation.10 | convolution fusion | flops 1213120512 | bytes 11846656 | tf_op jit(solution)/shard_map/dot_general | solution.py:38
  123.8 0.0 copy-done.5
  123.8 3.8 fusion.10
  127.7 1.9 multiply_reduce_fusion
  129.5 2.5 fusion.16
  132.1 0.0 copy-start.3
  132.1 0.0 copy-start.4
  132.1 82.5 %fusion = f32[40,768]{1,0:T(8,128)S(1)} fusion(f32[1152,768]{1,0:T(8,128)} %fusion.16), kind=kCustom, calls=%all-reduce-scatter | all-reduce-scatter fusion | flops 983041 | bytes 3663872
  214.6 4.1 collective-permute-start.3
  218.7 1.5 collective-permute-start.2
  220.2 2.9 collective-permute-start.1
  223.1 5.6 %collective-permute-start.4 = (f32[4,768]{1,0:T(4,128)S(1)}, f32[4,768]{1,0:T(4,128)S(1)}, u32[]{:S(2)}, u32[]{:S(2)}) collective-permute-start(f32[4,768]{1,0:T(4,128)S(1)} %slice), channel_id=1, source_target_pairs={{0,4},{1,5},{2,6},{3,7},{4,8},{5,9},{6,10},{7,11},{8,12},{9,13},{1... | collective-permute-start | bytes 36872
  228.7 1.3 dynamic-slice.6
  230.6 0.0 collective-permute-done.4
  230.6 0.0 collective-permute-done.3
  230.7 0.0 collective-permute-done.2
  230.7 0.0 collective-permute-done.1
  230.7 0.6 concatenate.4
  231.3 0.7 constant_dynamic-slice_fusion
  232.0 0.0 all-reduce.4.cloned.1.call-update
  232.0 0.0 all-gather.6.cloned.1.call-start
  232.1 149.7 %all-reduce.4.cloned.1.call-done = f32[36,768]{1,0:T(8,128)} async-done(((f32[36,768]{1,0:T(8,128)}), f32[36,768]{1,0:T(8,128)}) %all-reduce.4.cloned.1.call-update) | async-done | bytes 110608 | tf_op jit(solution)/shard_map/psum | solution.py:106
  381.7 0.0 copy-done.3
  381.7 0.0 copy-done.4
  381.7 1.7 fusion.26
  383.4 0.0 all-gather.6.cloned.1.call-update
  383.4 0.5 broadcast_multiply_fusion
  384.0 137.8 %all-gather.6.cloned.1.call-done = bf16[32,36,768]{2,1,0:T(8,128)(2,1)} async-done(((bf16[1,36,768]{2,1,0:T(8,128)(2,1)}), bf16[32,36,768]{2,1,0:T(8,128)(2,1)}) %all-gather.6.cloned.1.call-update) | async-done | bytes 1769488 | tf_op jit(solution)/shard_map/all_gather | solution.py:117
  521.8 3.6 reshape.37
  (5 shorter events, 0.0 us)
Async XLA Ops:
  7.2 15.8 %copy-start = (bf16[128,768]{1,0:T(8,128)(2,1)S(1)}, bf16[128,768]{1,0:T(8,128)(2,1)}, u32[]{:S(2)}) copy-start(bf16[128,768]{1,0:T(8,128)(2,1)} %param.7) | copy-start | bytes 589828
  7.2 15.6 %copy-start.2 = (bf16[128,1152]{1,0:T(8,128)(2,1)S(1)}, bf16[128,1152]{1,0:T(8,128)(2,1)}, u32[]{:S(2)}) copy-start(bf16[128,1152]{1,0:T(8,128)(2,1)} %param.8) | copy-start | bytes 884740
  7.2 15.8 %copy-start.1 = (bf16[1152,768]{1,0:T(8,128)(2,1)S(1)}, bf16[1152,768]{1,0:T(8,128)(2,1)}, u32[]{:S(2)}) copy-start(bf16[1152,768]{1,0:T(8,128)(2,1)} %param.11) | copy-start | bytes 5308420
  7.2 109.6 %all-gather.4.cloned.1.call-start = ((), (), s32[]{:S(2)}) async-start(), calls=%async_computation | async-start | bytes 10027008 | tf_op jit(solution)/shard_map/all_gather | solution.py:84
  9.6 10.6 %collective-permute-start = (bf16[128,1152]{1,0:T(8,128)(2,1)S(1)}, bf16[128,1152]{1,0:T(8,128)(2,1)S(1)}, u32[]{:S(2)}, u32[]{:S(2)}) collective-permute-start(bf16[128,1152]{1,0:T(8,128)(2,1)S(1)} %fusion.13), channel_id=1, source_target_pairs={{0,16},{1,17},{2,18},{3,19},{4,20},{5,21},{6,22},{7,23},{8,24},{9,... | collective-permute-start | bytes 884744 | tf_op jit(solution)/shard_map/ppermute | solution.py:21
  21.1 360.6 %all-reduce.4.cloned.1.call-start = ((), (), s32[]{:S(2)}) async-start(), calls=%async_computation.1 | async-start | bytes 245760 | tf_op jit(solution)/shard_map/psum | solution.py:106
  116.8 7.1 %copy-start.5 = (bf16[4096,1152]{1,0:T(8,128)(2,1)S(1)}, bf16[4096,1152]{1,0:T(8,128)(2,1)}, u32[]{:S(2)}) copy-start(bf16[4096,1152]{1,0:T(8,128)(2,1)} %all-gather.4.cloned.1.call-done) | copy-start | bytes 28311556
  132.1 249.7 %copy-start.3 = (f32[36,768]{1,0:T(8,128)S(1)}, f32[36,768]{1,0:T(8,128)}, u32[]{:S(2)}) copy-start(f32[36,768]{1,0:T(8,128)} %param.13) | copy-start | bytes 331780
  132.1 249.7 %copy-start.4 = (f32[36,768]{1,0:T(8,128)S(1)}, f32[36,768]{1,0:T(8,128)}, u32[]{:S(2)}) copy-start(f32[36,768]{1,0:T(8,128)} %param.12) | copy-start | bytes 331780
  214.6 16.1 %collective-permute-start.3 = (f32[40,768]{1,0:T(8,128)S(1)}, f32[40,768]{1,0:T(8,128)S(1)}, u32[]{:S(2)}, u32[]{:S(2)}) collective-permute-start(f32[40,768]{1,0:T(8,128)S(1)} %fusion), channel_id=1, source_target_pairs={{0,3},{1,4},{2,5},{3,6},{4,7},{5,8},{6,9},{7,10},{8,11},{9,12},{10... | collective-permute-start | bytes 368648
  218.7 12.0 %collective-permute-start.2 = (f32[40,768]{1,0:T(8,128)S(1)}, f32[40,768]{1,0:T(8,128)S(1)}, u32[]{:S(2)}, u32[]{:S(2)}) collective-permute-start(f32[40,768]{1,0:T(8,128)S(1)} %fusion), channel_id=1, source_target_pairs={{0,2},{1,3},{2,4},{3,5},{4,6},{5,7},{6,8},{7,9},{8,10},{9,11},{10,... | collective-permute-start | bytes 368648
  220.2 10.5 %collective-permute-start.1 = (f32[40,768]{1,0:T(8,128)S(1)}, f32[40,768]{1,0:T(8,128)S(1)}, u32[]{:S(2)}, u32[]{:S(2)}) collective-permute-start(f32[40,768]{1,0:T(8,128)S(1)} %fusion), channel_id=1, source_target_pairs={{0,1},{1,2},{2,3},{3,4},{4,5},{5,6},{6,7},{7,8},{8,9},{9,10},{10,1... | collective-permute-start | bytes 368648
  223.1 7.5 %collective-permute-start.4 = (f32[4,768]{1,0:T(4,128)S(1)}, f32[4,768]{1,0:T(4,128)S(1)}, u32[]{:S(2)}, u32[]{:S(2)}) collective-permute-start(f32[4,768]{1,0:T(4,128)S(1)} %slice), channel_id=1, source_target_pairs={{0,4},{1,5},{2,6},{3,7},{4,8},{5,9},{6,10},{7,11},{8,12},{9,13},{1... | collective-permute-start | bytes 36872
  232.0 289.8 %all-gather.6.cloned.1.call-start = ((), (), s32[]{:S(2)}) async-start(), calls=%async_computation.2 | async-start | bytes 2027520 | tf_op jit(solution)/shard_map/all_gather | solution.py:117
Sparse Core Ops, SparseCore 0:
  21.2 95.4 all-gather.3
  232.1 149.5 all-reduce.3
  384.4 137.3 all-gather.5
where the time goes:
time: 532 us
  waiting for transfers between devices  388 us (73%)
  blocking collectives  82.5 us (16%)
  starting transfers between devices  17.6 us (3%)
  matrix products  16.1 us (3%)
  between operations  14.6 us (3%)
  local copies, waits for them, and re-layouts  7.8 us (1%)
  other arithmetic  5.56 us (1%)
    psum x1, waiting for transfers between devices, per_device(): head_grad = lax.psum(group_grad, 'blk')  150 us
    all_gather x1, waiting for transfers between devices, per_device(): lax.all_gather(updated.astype(jnp.bfloat16), 'group', axis=0, tiled=True)  138 us
    all_gather x1, waiting for transfers between devices, per_device(): lax.all_gather(paired, 'blk', axis=0, tiled=True)  93 us
    unnamed x1, blocking collectives  82.5 us
    unnamed x4, starting transfers between devices  14.1 us
  transfers between devices with their start and end apart: 8, of which 4 were waited for; matrix products, arithmetic and copies ran while one was open for 1% of the time, Pallas kernels for 0%

commit v1 on v0

--- a/solution.py
+++ b/solution.py
@@ -103,7 +103,7 @@
         scatter_dimension=0,
         tiled=True,
     )
-    head_grad = lax.psum(group_grad, "blk")
+    head_grad = jnp.sum(lax.all_gather(group_grad, "blk"), axis=0)
     new_first = beta_one * moment_first + (1.0 - beta_one) * head_grad
     new_second = beta_two * moment_second + (1.0 - beta_two) * head_grad * head_grad
     first_hat = new_first / (1.0 - beta_one**adam_step)

time: 532 us -> 442 us (0.83)
  waiting for transfers between devices: 388 us -> 296 us
    psum x1 -> x0, waiting for transfers between devices: 150 us -> none  [per_device(): head_grad = lax.psum(group_grad, 'blk')]
    all_gather x0 -> x1, waiting for transfers between devices: none -> 63.9 us  [per_device(): head_grad = jnp.sum(lax.all_gather(group_grad, 'blk'), axis=0)]
    all_gather x1, waiting for transfers between devices: 138 us -> 132 us  [per_device(): lax.all_gather(updated.astype(jnp.bfloat16), 'group', axis=0, tiled=True)]
where the time goes in v1:
time: 442 us; the launch traced here: 441 us
  waiting for transfers between devices  296 us (67%)
  blocking collectives  82.5 us (19%)
  starting transfers between devices  17.8 us (4%)
  matrix products  16.1 us (4%)
  between operations  14.6 us (3%)
  local copies, waits for them, and re-layouts  7.81 us (2%)
  other arithmetic  6.32 us (1%)
    all_gather x1, waiting for transfers between devices, per_device(): lax.all_gather(updated.astype(jnp.bfloat16), 'group', axis=0, tiled=True)  132 us
    all_gather x1, waiting for transfers between devices, per_device(): lax.all_gather(paired, 'blk', axis=0, tiled=True)  93 us
    unnamed x1, blocking collectives  82.5 us
    all_gather x1, waiting for transfers between devices, per_device(): head_grad = jnp.sum(lax.all_gather(group_grad, 'blk'), axis=0)  63.9 us
    unnamed x4, starting transfers between devices  14.3 us
  transfers between devices with their start and end apart: 8, of which 4 were waited for; matrix products, arithmetic and copies ran while one was open for 1% of the time, Pallas kernels for 0%

profile of v1, /device:TPU:8, one launch (start us, length us, event | category | flops | bytes accessed | tf_op | source)
XLA Modules:
  0.0 441.5 jit_solution(6610632112047682264)
XLA Ops:
  7.2 0.0 copy-start
  7.2 0.0 copy-start.2
  7.2 0.0 copy-start.1
  7.2 0.0 all-gather.7.cloned.1.call-start
  7.2 1.3 fusion.12
  8.5 1.1 fusion.13
  9.6 3.4 collective-permute-start
  13.0 7.2 %collective-permute-done = bf16[128,1152]{1,0:T(8,128)(2,1)S(1)} collective-permute-done((bf16[128,1152]{1,0:T(8,128)(2,1)S(1)}, bf16[128,1152]{1,0:T(8,128)(2,1)S(1)}, u32[]{:S(2)}, u32[]{:S(2)}) %collective-permute-start) | collective-permute-done | bytes 294944 | tf_op jit(solution)/shard_map/ppermute | solution.py:21
  20.2 0.9 pad_maximum_fusion
  21.1 0.0 all-gather.7.cloned.1.call-update
  21.1 0.0 all-gather.9.cloned.1.call-start
  21.2 0.7 fusion.27
  21.9 0.9 constant_dynamic-slice_fusion.1
  22.8 0.0 copy-done.2
  22.8 0.1 fusion.14
  23.0 0.0 copy-done
  23.0 0.0 copy-done.1
  23.0 0.8 multiply_reduce_fusion.1
  23.8 93.0 %all-gather.7.cloned.1.call-done = bf16[4096,1152]{1,0:T(8,128)(2,1)} async-done(((bf16[256,1152]{1,0:T(8,128)(2,1)}), bf16[4096,1152]{1,0:T(8,128)(2,1)}) %all-gather.7.cloned.1.call-update) | async-done | bytes 9437200 | tf_op jit(solution)/shard_map/all_gather | solution.py:84
  116.8 0.0 copy-start.5
  116.8 7.1 %fusion.8 = f32[128,4096]{1,0:T(8,128)S(1)} fusion(bf16[4096,1152]{1,0:T(8,128)(2,1)} %all-gather.7.cloned.1.call-done, s32[4096]{0:T(1024)S(1)} %bitcast.17, s32[128]{0:T(128)S(1)} %fusion.27, bf16[128,1152]{1,0:T(8,128)(2,1)S(1)} %copy-done.2, f32[128]{0:T(128)S(1)} %add_rsqrt_fusion), kind=kOutput, calls=%fused_computation.10 | convolution fusion | flops 1213120512 | bytes 11846656 | tf_op jit(solution)/shard_map/dot_general | solution.py:38
  123.8 0.0 copy-done.5
  123.8 3.8 fusion.10
  127.7 1.9 multiply_reduce_fusion
  129.5 2.5 fusion.16
  132.1 82.5 %fusion = f32[40,768]{1,0:T(8,128)S(1)} fusion(f32[1152,768]{1,0:T(8,128)} %fusion.16), kind=kCustom, calls=%all-reduce-scatter | all-reduce-scatter fusion | flops 983041 | bytes 3663872
  214.5 0.0 copy-start.3
  214.6 0.0 copy-start.4
  214.6 4.2 collective-permute-start.3
  218.8 2.0 collective-permute-start.2
  220.8 2.4 collective-permute-start.1
  223.2 5.7 %collective-permute-start.4 = (f32[4,768]{1,0:T(4,128)S(1)}, f32[4,768]{1,0:T(4,128)S(1)}, u32[]{:S(2)}, u32[]{:S(2)}) collective-permute-start(f32[4,768]{1,0:T(4,128)S(1)} %slice), channel_id=1, source_target_pairs={{0,4},{1,5},{2,6},{3,7},{4,8},{5,9},{6,10},{7,11},{8,12},{9,13},{1... | collective-permute-start | bytes 36872
  228.9 1.3 dynamic-slice.6
  230.8 0.0 collective-permute-done.4
  230.8 0.0 collective-permute-done.3
  230.8 0.0 collective-permute-done.2
  230.8 0.0 collective-permute-done.1
  230.9 0.6 concatenate.4
  231.5 0.7 dynamic-slice_bitcast_fusion
  232.2 0.0 all-gather.9.cloned.1.call-update
  232.2 0.0 all-gather.11.cloned.1.call-start
  232.2 63.9 %all-gather.9.cloned.1.call-done = f32[16,36,768]{2,1,0:T(8,128)} async-done(((f32[1,36,768]{2,1,0:T(8,128)}), f32[16,36,768]{2,1,0:T(8,128)}) %all-gather.9.cloned.1.call-update) | async-done | bytes 1769488 | tf_op jit(solution)/shard_map/all_gather | solution.py:106
  296.1 1.6 reduce_sum.59
  297.8 0.0 copy-done.3
  297.8 0.0 copy-done.4
  297.8 0.8 fusion.26
  298.6 0.0 all-gather.11.cloned.1.call-update
  298.6 0.5 broadcast_multiply_fusion
  299.1 132.2 %all-gather.11.cloned.1.call-done = bf16[32,36,768]{2,1,0:T(8,128)(2,1)} async-done(((bf16[1,36,768]{2,1,0:T(8,128)(2,1)}), bf16[32,36,768]{2,1,0:T(8,128)(2,1)}) %all-gather.11.cloned.1.call-update) | async-done | bytes 1769488 | tf_op jit(solution)/shard_map/all_gather | solution.py:117
  431.3 3.6 reshape.40
  (5 shorter events, 0.0 us)
Async XLA Ops:
  7.2 15.8 %copy-start = (bf16[128,768]{1,0:T(8,128)(2,1)S(1)}, bf16[128,768]{1,0:T(8,128)(2,1)}, u32[]{:S(2)}) copy-start(bf16[128,768]{1,0:T(8,128)(2,1)} %param.7) | copy-start | bytes 589828
  7.2 15.6 %copy-start.2 = (bf16[128,1152]{1,0:T(8,128)(2,1)S(1)}, bf16[128,1152]{1,0:T(8,128)(2,1)}, u32[]{:S(2)}) copy-start(bf16[128,1152]{1,0:T(8,128)(2,1)} %param.8) | copy-start | bytes 884740
  7.2 15.8 %copy-start.1 = (bf16[1152,768]{1,0:T(8,128)(2,1)S(1)}, bf16[1152,768]{1,0:T(8,128)(2,1)}, u32[]{:S(2)}) copy-start(bf16[1152,768]{1,0:T(8,128)(2,1)} %param.11) | copy-start | bytes 5308420
  7.2 109.6 %all-gather.7.cloned.1.call-start = ((), (), s32[]{:S(2)}) async-start(), calls=%async_computation | async-start | bytes 10027008 | tf_op jit(solution)/shard_map/all_gather | solution.py:84
  9.6 10.6 %collective-permute-start = (bf16[128,1152]{1,0:T(8,128)(2,1)S(1)}, bf16[128,1152]{1,0:T(8,128)(2,1)S(1)}, u32[]{:S(2)}, u32[]{:S(2)}) collective-permute-start(bf16[128,1152]{1,0:T(8,128)(2,1)S(1)} %fusion.13), channel_id=1, source_target_pairs={{0,16},{1,17},{2,18},{3,19},{4,20},{5,21},{6,22},{7,23},{8,24},{9,... | collective-permute-start | bytes 884744 | tf_op jit(solution)/shard_map/ppermute | solution.py:21
  21.1 275.0 %all-gather.9.cloned.1.call-start = ((), (), s32[]{:S(2)}) async-start(), calls=%async_computation.1 | async-start | bytes 2088960 | tf_op jit(solution)/shard_map/all_gather | solution.py:106
  116.8 7.1 %copy-start.5 = (bf16[4096,1152]{1,0:T(8,128)(2,1)S(1)}, bf16[4096,1152]{1,0:T(8,128)(2,1)}, u32[]{:S(2)}) copy-start(bf16[4096,1152]{1,0:T(8,128)(2,1)} %all-gather.7.cloned.1.call-done) | copy-start | bytes 28311556
  214.5 83.3 %copy-start.3 = (f32[36,768]{1,0:T(8,128)S(1)}, f32[36,768]{1,0:T(8,128)}, u32[]{:S(2)}) copy-start(f32[36,768]{1,0:T(8,128)} %param.13) | copy-start | bytes 331780
  214.6 83.2 %copy-start.4 = (f32[36,768]{1,0:T(8,128)S(1)}, f32[36,768]{1,0:T(8,128)}, u32[]{:S(2)}) copy-start(f32[36,768]{1,0:T(8,128)} %param.12) | copy-start | bytes 331780
  214.6 16.3 %collective-permute-start.3 = (f32[40,768]{1,0:T(8,128)S(1)}, f32[40,768]{1,0:T(8,128)S(1)}, u32[]{:S(2)}, u32[]{:S(2)}) collective-permute-start(f32[40,768]{1,0:T(8,128)S(1)} %fusion), channel_id=1, source_target_pairs={{0,3},{1,4},{2,5},{3,6},{4,7},{5,8},{6,9},{7,10},{8,11},{9,12},{10... | collective-permute-start | bytes 368648
  218.8 12.1 %collective-permute-start.2 = (f32[40,768]{1,0:T(8,128)S(1)}, f32[40,768]{1,0:T(8,128)S(1)}, u32[]{:S(2)}, u32[]{:S(2)}) collective-permute-start(f32[40,768]{1,0:T(8,128)S(1)} %fusion), channel_id=1, source_target_pairs={{0,2},{1,3},{2,4},{3,5},{4,6},{5,7},{6,8},{7,9},{8,10},{9,11},{10,... | collective-permute-start | bytes 368648
  220.8 10.1 %collective-permute-start.1 = (f32[40,768]{1,0:T(8,128)S(1)}, f32[40,768]{1,0:T(8,128)S(1)}, u32[]{:S(2)}, u32[]{:S(2)}) collective-permute-start(f32[40,768]{1,0:T(8,128)S(1)} %fusion), channel_id=1, source_target_pairs={{0,1},{1,2},{2,3},{3,4},{4,5},{5,6},{6,7},{7,8},{8,9},{9,10},{10,1... | collective-permute-start | bytes 368648
  223.2 7.6 %collective-permute-start.4 = (f32[4,768]{1,0:T(4,128)S(1)}, f32[4,768]{1,0:T(4,128)S(1)}, u32[]{:S(2)}, u32[]{:S(2)}) collective-permute-start(f32[4,768]{1,0:T(4,128)S(1)} %slice), channel_id=1, source_target_pairs={{0,4},{1,5},{2,6},{3,7},{4,8},{5,9},{6,10},{7,11},{8,12},{9,13},{1... | collective-permute-start | bytes 36872
  232.2 199.1 %all-gather.11.cloned.1.call-start = ((), (), s32[]{:S(2)}) async-start(), calls=%async_computation.2 | async-start | bytes 2027520 | tf_op jit(solution)/shard_map/all_gather | solution.py:117
Sparse Core Ops, SparseCore 0:
  21.2 95.4 all-gather.6
  232.3 63.7 all-gather.8
  298.8 132.4 all-gather.10
